TPU v7x, 128 devices: a whole 4x4x4 slice. The times are simulated.
128 devices in a mesh: store: 8 (over z, core), mp: 16 (over y, x).
Axes of the slice: x: 4, y: 4, z: 4, core: 2. Of those that a mesh axis runs over, the one named last changes fastest.
Arguments:
- tokens: bfloat16 [2048, 6144], P('store', 'mp'), may hold values from -6 to 6
- gain: float32 [6144], replicated, may hold values from 0.1 to 1.9
- base_projection_weight: bfloat16 [6144, 6144], P(None, 'mp'), may hold values from -0.078125 to 0.078125
- adapter_down_weight: bfloat16 [64, 64, 6144], P('store', None, 'mp'), may hold values from -0.078125 to 0.078125
- adapter_up_weight: bfloat16 [64, 64, 6144], P('store', None, 'mp'), may hold values from -0.75 to 0.75
- plan: int32 [8, 4], replicated, may hold values from 0 to 63, as said below
- target: int32 [2048, 1], P('store'), may hold values from 0 to 7; in each aligned block of 256 rows (0 to 255, 256 to 511, ...) at most 64 rows name the same one
- slot: int32 [2048], P('store'), may hold values from 0 to 11
Outputs:
- hidden_out: bfloat16 [2048, 6144], P('store', 'mp')
Inputs may be any that keep to these rules, and one draw needn't show every extreme that they name: plan[g, r] is an adapter owned by a store group other than g; adapter a is owned by group a // 8. `target`: among the 256 rows of one store group at most 64 name the same group, a bound that some block reaches.
All inputs are finite; a program needn't handle non-finite values.
Results may differ from a plain program's by a relative error of at most 0.0063.
Values may be sent and summed in bfloat16 or wider, within the bound.
A program may use at most 64 MiB of HBM per device.

v0:
```python
import jax
import jax.numpy as jnp
from jax import lax
from jax.sharding import PartitionSpec as P

STEPS = 4
CAP = 64


adapter_scale = 0.5


def local(
    tokens, gain, base_projection_weight, adapter_down_weight, adapter_up_weight, plan, target, slot
):
    store_count = lax.axis_size("store")
    group = lax.axis_index("store")
    owned_adapters = adapter_down_weight.shape[0]
    rank_position = adapter_down_weight.shape[1]
    width_portion = adapter_down_weight.shape[2]
    replica_count = plan.shape[1]
    n_slots = owned_adapters + replica_count
    flattened_down = adapter_down_weight.reshape(owned_adapters, rank_position * width_portion)
    flattened_up = adapter_up_weight.reshape(owned_adapters, rank_position * width_portion)
    own_plan = lax.dynamic_slice_in_dim(plan, group, 1, 0)[0]
    pieces = (
        lax.all_gather(flattened_down, "store", axis=0, tiled=True),
        lax.all_gather(flattened_up, "store", axis=0, tiled=True),
    )
    count = pieces[0].shape[0]
    select = (own_plan[:, None] == jnp.arange(count, dtype=jnp.int32)[None, :]).astype(jnp.bfloat16)
    replica_down_factor = jnp.dot(select, pieces[0], preferred_element_type=jnp.float32)
    replica_up_factor = jnp.dot(select, pieces[1], preferred_element_type=jnp.float32)
    host_down = jnp.concatenate(
        [
            adapter_down_weight,
            replica_down_factor.astype(jnp.bfloat16).reshape(
                replica_count, rank_position, width_portion
            ),
        ],
        0,
    )
    host_down = host_down.reshape(n_slots * rank_position, width_portion)
    host_up = jnp.concatenate(
        [
            adapter_up_weight,
            replica_up_factor.astype(jnp.bfloat16).reshape(
                replica_count, rank_position, width_portion
            ),
        ],
        0,
    )
    host_up = host_up.reshape(n_slots * rank_position, width_portion)
    target_group = target[:, 0]
    member = (target_group[:, None] == jnp.arange(store_count, dtype=jnp.int32)[None, :]).astype(
        jnp.int32
    )
    earlier = jnp.cumsum(member, axis=0) - member
    bucket_place = jnp.sum(earlier * member, axis=1)
    row_index = target_group * CAP + bucket_place
    slot_buffer = (
        jnp.full((store_count * CAP,), -1, jnp.int32)
        .at[row_index]
        .set(slot)
        .reshape(store_count, CAP)
    )
    state = tokens
    column_start = lax.axis_index("mp") * width_portion
    for step in range(STEPS):
        whole = lax.all_gather(state, "mp", axis=1, tiled=True)
        values = whole.astype(jnp.float32)
        mean_sq = jnp.mean(values * values, axis=1, keepdims=True)
        normed = (values * lax.rsqrt(mean_sq + 1e-05) * gain[None, :]).astype(jnp.bfloat16)
        mine = lax.dynamic_slice_in_dim(normed, column_start, width_portion, 1)
        row_buffer = (
            jnp.zeros((store_count * CAP, width_portion), jnp.bfloat16).at[row_index].set(mine)
        )
        row_buffer = row_buffer.reshape(store_count, CAP, width_portion)
        rows = lax.all_to_all(row_buffer, "store", split_axis=0, concat_axis=0, tiled=True)
        slots_in = lax.all_to_all(slot_buffer, "store", split_axis=0, concat_axis=0, tiled=True)
        senders, adapter_count = slots_in.shape
        total_rows = senders * adapter_count
        flat_rows = rows.reshape(total_rows, width_portion)
        partial_value = lax.dot_general(
            flat_rows, host_down, (((1,), (1,)), ((), ())), preferred_element_type=jnp.float32
        )
        selected_adapter = (
            slots_in.reshape(total_rows)[:, None] == jnp.arange(n_slots, dtype=jnp.int32)[None, :]
        )
        partial_value = jnp.sum(
            partial_value.reshape(total_rows, n_slots, rank_position)
            * selected_adapter[:, :, None].astype(jnp.float32),
            axis=1,
        )
        summed_share = lax.psum_scatter(
            partial_value, "mp", scatter_dimension=0, tiled=True
        ).astype(jnp.bfloat16)
        inner = lax.all_gather(summed_share, "mp", axis=0, tiled=True)
        spread_rows = (
            selected_adapter[:, :, None].astype(jnp.bfloat16) * inner[:, None, :]
        ).reshape(total_rows, n_slots * rank_position)
        outer = jnp.dot(spread_rows, host_up, preferred_element_type=jnp.float32)
        outer = (
            (adapter_scale * outer)
            .astype(jnp.bfloat16)
            .reshape(senders, adapter_count, width_portion)
        )
        returned = lax.all_to_all(outer, "store", split_axis=0, concat_axis=0, tiled=True)
        delta = returned.reshape(store_count * CAP, width_portion)[row_index]
        base = jnp.dot(normed, base_projection_weight, preferred_element_type=jnp.float32)
        state = (state.astype(jnp.float32) + base + delta.astype(jnp.float32)).astype(jnp.bfloat16)
    return state


def solution(mesh):
    return jax.shard_map(
        local,
        mesh=mesh,
        in_specs=(
            P("store", "mp"),
            P(),
            P(None, "mp"),
            P("store", None, "mp"),
            P("store", None, "mp"),
            P(),
            P("store", None),
            P("store"),
        ),
        out_specs=P("store", "mp"),
        check_vma=False,
    )
```

profile of v0, /device:TPU:0, one launch (start us, length us, event | category | flops | bytes accessed | tf_op | source)
XLA Modules:
  0.0 812.9 jit_solution(17470650637500841050)
XLA Ops:
  16.6 5.4 all-to-all-start
  29.1 34.5 %all-gather.7.cloned.1.call-done = bf16[256,6144]{1,0:T(8,128)(2,1)} async-done(((bf16[256,384]{1,0:T(8,128)(2,1)}), bf16[256,6144]{1,0:T(8,128)(2,1)}) %all-gather.7.cloned.1.call-update) | async-done | bytes 3145744 | tf_op jit(solution)/shard_map/all_gather | solution.py:70
  75.0 21.9 %all-gather.9.cloned.1.call-done = bf16[64,24576]{1,0:T(8,128)(2,1)} async-done(((bf16[8,24576]{1,0:T(8,128)(2,1)}), bf16[64,24576]{1,0:T(8,128)(2,1)}) %all-gather.9.cloned.1.call-update) | async-done | bytes 3145744 | tf_op jit(solution)/shard_map/all_gather | solution.py:27
  104.2 20.9 %all-gather.11.cloned.1.call-done = bf16[64,24576]{1,0:T(8,128)(2,1)} async-done(((bf16[8,24576]{1,0:T(8,128)(2,1)}), bf16[64,24576]{1,0:T(8,128)(2,1)}) %all-gather.11.cloned.1.call-update) | async-done | bytes 3145744 | tf_op jit(solution)/shard_map/all_gather | solution.py:28
  128.3 72.8 %reduce-scatter.13.cloned.1.call-done = f32[32,64]{1,0:T(8,128)} async-done(((f32[512,64]{1,0:T(8,128)}), f32[32,64]{1,0:T(8,128)}) %reduce-scatter.13.cloned.1.call-update) | async-done | bytes 8208 | tf_op jit(solution)/shard_map/reduce_scatter | solution.py:95
  201.9 23.0 %all_gather.32 = bf16[512,64]{1,0:T(8,128)(2,1)S(1)} all-gather(bf16[32,64]{1,0:T(8,128)(2,1)S(1)} %convert_element_type.128), channel_id=1, replica_groups=mesh['store'=8,'mp'=16] {'mp'}, dimensions={0}, use_global_device_ids=true | all-gather | bytes 69632 | tf_op jit(solution)/shard_map/all_gather | solution.py:98
  231.9 8.9 %all-to-all-done.2 = bf16[8,64,384]{2,1,0:T(8,128)(2,1)S(1)} async-done(((bf16[8,64,384]{2,1,0:T(8,128)(2,1)}), bf16[8,64,384]{2,1,0:T(8,128)(2,1)S(1)}, u32[]{:S(2)}, u32[]{:S(2)}) %all-to-all-start.2) | async-done | bytes 393248 | tf_op jit(solution)/shard_map/all_to_all | solution.py:108
  247.9 48.4 %all-gather.13.cloned.1.call-done = bf16[256,6144]{1,0:T(8,128)(2,1)} async-done(((bf16[256,384]{1,0:T(8,128)(2,1)}), bf16[256,6144]{1,0:T(8,128)(2,1)}) %all-gather.13.cloned.1.call-update) | async-done | bytes 3145744 | tf_op jit(solution)/shard_map/all_gather | solution.py:70
  301.8 13.1 %all_to_all.52 = bf16[8,64,384]{2,1,0:T(8,128)(2,1)S(1)} all-to-all(bf16[8,64,384]{2,1,0:T(8,128)(2,1)S(1)} %bitcast.110), channel_id=1, replica_groups=mesh['store'=8,'mp'=16] {'store'}, dimensions={0} | all-to-all | bytes 786432 | tf_op jit(solution)/shard_map/all_to_all | solution.py:79
  317.6 70.7 %reduce-scatter.15.cloned.1.call-done = f32[32,64]{1,0:T(8,128)} async-done(((f32[512,64]{1,0:T(8,128)}), f32[32,64]{1,0:T(8,128)}) %reduce-scatter.15.cloned.1.call-update) | async-done | bytes 8208 | tf_op jit(solution)/shard_map/reduce_scatter | solution.py:95
  389.0 23.0 %all_gather.35 = bf16[512,64]{1,0:T(8,128)(2,1)S(1)} all-gather(bf16[32,64]{1,0:T(8,128)(2,1)S(1)} %convert_element_type.136), channel_id=1, replica_groups=mesh['store'=8,'mp'=16] {'mp'}, dimensions={0}, use_global_device_ids=true | all-gather | bytes 69632 | tf_op jit(solution)/shard_map/all_gather | solution.py:98
  413.8 13.1 %all_to_all.53 = bf16[8,64,384]{2,1,0:T(8,128)(2,1)S(1)} all-to-all(bf16[8,64,384]{2,1,0:T(8,128)(2,1)S(1)} %bitcast.119), channel_id=1, replica_groups=mesh['store'=8,'mp'=16] {'store'}, dimensions={0} | all-to-all | bytes 786432 | tf_op jit(solution)/shard_map/all_to_all | solution.py:108
  428.7 5.0 fusion.26
  433.8 48.6 %all-gather.15.cloned.1.call-done = bf16[256,6144]{1,0:T(8,128)(2,1)} async-done(((bf16[256,384]{1,0:T(8,128)(2,1)}), bf16[256,6144]{1,0:T(8,128)(2,1)}) %all-gather.15.cloned.1.call-update) | async-done | bytes 3145744 | tf_op jit(solution)/shard_map/all_gather | solution.py:70
  488.0 13.1 %all_to_all.54 = bf16[8,64,384]{2,1,0:T(8,128)(2,1)S(1)} all-to-all(bf16[8,64,384]{2,1,0:T(8,128)(2,1)S(1)} %bitcast.111), channel_id=1, replica_groups=mesh['store'=8,'mp'=16] {'store'}, dimensions={0} | all-to-all | bytes 786432 | tf_op jit(solution)/shard_map/all_to_all | solution.py:79
  503.7 70.7 %reduce-scatter.17.cloned.1.call-done = f32[32,64]{1,0:T(8,128)} async-done(((f32[512,64]{1,0:T(8,128)}), f32[32,64]{1,0:T(8,128)}) %reduce-scatter.17.cloned.1.call-update) | async-done | bytes 8208 | tf_op jit(solution)/shard_map/reduce_scatter | solution.py:95
  575.1 23.0 %all_gather.37 = bf16[512,64]{1,0:T(8,128)(2,1)S(1)} all-gather(bf16[32,64]{1,0:T(8,128)(2,1)S(1)} %convert_element_type.143), channel_id=1, replica_groups=mesh['store'=8,'mp'=16] {'mp'}, dimensions={0}, use_global_device_ids=true | all-gather | bytes 69632 | tf_op jit(solution)/shard_map/all_gather | solution.py:98
  599.9 13.1 %all_to_all.55 = bf16[8,64,384]{2,1,0:T(8,128)(2,1)S(1)} all-to-all(bf16[8,64,384]{2,1,0:T(8,128)(2,1)S(1)} %bitcast.121), channel_id=1, replica_groups=mesh['store'=8,'mp'=16] {'store'}, dimensions={0} | all-to-all | bytes 786432 | tf_op jit(solution)/shard_map/all_to_all | solution.py:108
  614.9 5.0 fusion.25
  620.0 48.6 %all-gather.17.cloned.1.call-done = bf16[256,6144]{1,0:T(8,128)(2,1)} async-done(((bf16[256,384]{1,0:T(8,128)(2,1)}), bf16[256,6144]{1,0:T(8,128)(2,1)}) %all-gather.17.cloned.1.call-update) | async-done | bytes 3145744 | tf_op jit(solution)/shard_map/all_gather | solution.py:70
  674.1 13.1 %all_to_all.56 = bf16[8,64,384]{2,1,0:T(8,128)(2,1)S(1)} all-to-all(bf16[8,64,384]{2,1,0:T(8,128)(2,1)S(1)} %bitcast.109), channel_id=1, replica_groups=mesh['store'=8,'mp'=16] {'store'}, dimensions={0} | all-to-all | bytes 786432 | tf_op jit(solution)/shard_map/all_to_all | solution.py:79
  689.8 70.7 %reduce-scatter.19.cloned.1.call-done = f32[32,64]{1,0:T(8,128)} async-done(((f32[512,64]{1,0:T(8,128)}), f32[32,64]{1,0:T(8,128)}) %reduce-scatter.19.cloned.1.call-update) | async-done | bytes 8208 | tf_op jit(solution)/shard_map/reduce_scatter | solution.py:95
  761.2 23.0 %all_gather.39 = bf16[512,64]{1,0:T(8,128)(2,1)S(1)} all-gather(bf16[32,64]{1,0:T(8,128)(2,1)S(1)} %convert_element_type.150), channel_id=1, replica_groups=mesh['store'=8,'mp'=16] {'mp'}, dimensions={0}, use_global_device_ids=true | all-gather | bytes 69632 | tf_op jit(solution)/shard_map/all_gather | solution.py:98
  786.1 13.1 %all_to_all.57 = bf16[8,64,384]{2,1,0:T(8,128)(2,1)S(1)} all-to-all(bf16[8,64,384]{2,1,0:T(8,128)(2,1)S(1)} %bitcast.117), channel_id=1, replica_groups=mesh['store'=8,'mp'=16] {'store'}, dimensions={0} | all-to-all | bytes 786432 | tf_op jit(solution)/shard_map/all_to_all | solution.py:108
  (115 shorter events, 96.0 us)
Async XLA Ops:
  6.5 18.1 %copy-start = (s32[8,4]{0,1:T(4,128)S(1)}, s32[8,4]{0,1:T(4,128)}, u32[]{:S(2)}) copy-start(s32[8,4]{0,1:T(4,128)} %param.13) | copy-start | bytes 388
  6.5 17.3 %copy-start.5 = (bf16[8,64,384]{2,1,0:T(8,128)(2,1)S(1)}, bf16[8,64,384]{2,1,0:T(8,128)(2,1)}, u32[]{:S(2)}) copy-start(bf16[8,64,384]{2,1,0:T(8,128)(2,1)} %param.12) | copy-start | bytes 1179652
  6.5 57.1 %all-gather.7.cloned.1.call-start = ((), (), s32[]{:S(2)}) async-start(), calls=%async_computation.13 | async-start | bytes 3342336 | tf_op jit(solution)/shard_map/all_gather | solution.py:70
  7.3 89.6 %all-gather.9.cloned.1.call-start = ((), (), s32[]{:S(2)}) async-start(), calls=%async_computation.14 | async-start | bytes 3538944 | tf_op jit(solution)/shard_map/all_gather | solution.py:27
  9.3 115.8 %all-gather.11.cloned.1.call-start = ((), (), s32[]{:S(2)}) async-start(), calls=%async_computation.15 | async-start | bytes 3538944 | tf_op jit(solution)/shard_map/all_gather | solution.py:28
  16.6 10.6 %all-to-all-start = ((s32[8,1,64]{2,1,0:T(1,128)}), s32[8,1,64]{2,1,0:T(1,128)S(1)}, u32[]{:S(2)}, u32[]{:S(2)}) async-start(s32[8,1,64]{2,1,0:T(1,128)} %all_to_all.33), calls=%async_computation | async-start | bytes 8192 | tf_op jit(solution)/shard_map/all_to_all | solution.py:80
  63.7 2.8 copy-start.1
  70.6 29.5 %all-to-all-start.1 = ((bf16[8,64,384]{2,1,0:T(8,128)(2,1)}), bf16[8,64,384]{2,1,0:T(8,128)(2,1)S(1)}, u32[]{:S(2)}, u32[]{:S(2)}) async-start(bf16[8,64,384]{2,1,0:T(8,128)(2,1)} %bitcast.6), calls=%async_computation.1 | async-start | bytes 786432 | tf_op jit(solution)/shard_map/all_to_all | solution.py:79
  75.0 126.1 %reduce-scatter.13.cloned.1.call-start = ((), (), s32[]{:S(2)}) async-start(), calls=%async_computation.19 | async-start | bytes 278528 | tf_op jit(solution)/shard_map/reduce_scatter | solution.py:95
  102.4 122.6 %copy-start.9 = (bf16[512,12]{0,1:T(8,128)(2,1)S(1)}, bf16[512,12]{0,1:T(8,128)(2,1)}, u32[]{:S(2)}) copy-start(bf16[512,12]{0,1:T(8,128)(2,1)} %get-tuple-element.5) | copy-start | bytes 36868
  227.4 13.3 %all-to-all-start.2 = ((bf16[8,64,384]{2,1,0:T(8,128)(2,1)}), bf16[8,64,384]{2,1,0:T(8,128)(2,1)S(1)}, u32[]{:S(2)}, u32[]{:S(2)}) async-start(bf16[8,64,384]{2,1,0:T(8,128)(2,1)} %bitcast.115), calls=%async_computation.2 | async-start | bytes 786432 | tf_op jit(solution)/shard_map/all_to_all | solution.py:108
  231.9 64.4 %all-gather.13.cloned.1.call-start = ((), (), s32[]{:S(2)}) async-start(), calls=%async_computation.16 | async-start | bytes 3342336 | tf_op jit(solution)/shard_map/all_gather | solution.py:70
  247.6 51.4 %copy-start.6 = (f32[6144]{0:T(1024)S(1)}, f32[6144]{0:T(1024)}, u32[]{:S(2)}) copy-start(f32[6144]{0:T(1024)} %param.9) | copy-start | bytes 73732
  247.6 140.6 %reduce-scatter.15.cloned.1.call-start = ((), (), s32[]{:S(2)}) async-start(), calls=%async_computation.20 | async-start | bytes 278528 | tf_op jit(solution)/shard_map/reduce_scatter | solution.py:95
  296.3 2.8 copy-start.2
  315.0 97.1 %copy-start.10 = (bf16[512,12]{0,1:T(8,128)(2,1)S(1)}, bf16[512,12]{0,1:T(8,128)(2,1)}, u32[]{:S(2)}) copy-start(bf16[512,12]{0,1:T(8,128)(2,1)} %get-tuple-element.5) | copy-start | bytes 36868
  317.5 164.9 %all-gather.15.cloned.1.call-start = ((), (), s32[]{:S(2)}) async-start(), calls=%async_computation.17 | async-start | bytes 3342336 | tf_op jit(solution)/shard_map/all_gather | solution.py:70
  433.8 51.4 %copy-start.7 = (f32[6144]{0:T(1024)S(1)}, f32[6144]{0:T(1024)}, u32[]{:S(2)}) copy-start(f32[6144]{0:T(1024)} %param.9) | copy-start | bytes 73732
  433.8 140.6 %reduce-scatter.17.cloned.1.call-start = ((), (), s32[]{:S(2)}) async-start(), calls=%async_computation.21 | async-start | bytes 278528 | tf_op jit(solution)/shard_map/reduce_scatter | solution.py:95
  501.1 97.1 %copy-start.11 = (bf16[512,12]{0,1:T(8,128)(2,1)S(1)}, bf16[512,12]{0,1:T(8,128)(2,1)}, u32[]{:S(2)}) copy-start(bf16[512,12]{0,1:T(8,128)(2,1)} %get-tuple-element.5) | copy-start | bytes 36868
  503.7 164.9 %all-gather.17.cloned.1.call-start = ((), (), s32[]{:S(2)}) async-start(), calls=%async_computation.18 | async-start | bytes 3342336 | tf_op jit(solution)/shard_map/all_gather | solution.py:70
  619.9 51.4 %copy-start.8 = (f32[6144]{0:T(1024)S(1)}, f32[6144]{0:T(1024)}, u32[]{:S(2)}) copy-start(f32[6144]{0:T(1024)} %param.9) | copy-start | bytes 73732
  619.9 140.6 %reduce-scatter.19.cloned.1.call-start = ((), (), s32[]{:S(2)}) async-start(), calls=%async_computation.22 | async-start | bytes 278528 | tf_op jit(solution)/shard_map/reduce_scatter | solution.py:95
  687.3 97.1 %copy-start.12 = (bf16[512,12]{0,1:T(8,128)(2,1)S(1)}, bf16[512,12]{0,1:T(8,128)(2,1)}, u32[]{:S(2)}) copy-start(bf16[512,12]{0,1:T(8,128)(2,1)} %get-tuple-element.5) | copy-start | bytes 36868
  (2 other events, 5.7 us)
Sparse Core Ops, SparseCore 0:
  9.4 54.1 all-gather.6
  65.3 31.5 all-gather.8
  98.6 26.5 all-gather.10
  128.2 72.9 reduce-scatter.12
  247.8 48.4 all-gather.12
  317.6 70.5 reduce-scatter.14
  433.9 48.4 all-gather.14
  503.8 70.5 reduce-scatter.16
  620.1 48.4 all-gather.16
  689.9 70.5 reduce-scatter.18
where the time goes:
time: 815 us; the launch traced here: 813 us
  waiting for transfers between devices  520 us (64%)
  blocking collectives  171 us (21%)
  matrix products  39.8 us (5%)
  local copies, waits for them, and re-layouts  30.5 us (4%)
  other arithmetic  23 us (3%)
  starting transfers between devices  14.8 us (2%)
  between operations  13.8 us (2%)
    reduce_scatter x4, waiting for transfers between devices, local(): lax.psum_scatter(partial_value, 'mp', scatter_dimension=0, tiled=True)  285 us
    all_gather x4, waiting for transfers between devices, local(): whole = lax.all_gather(state, 'mp', axis=1, tiled=True)  180 us
    all_gather x4, blocking collectives, local(): inner = lax.all_gather(summed_share, 'mp', axis=0, tiled=True)  92.2 us
    all_to_all x3, blocking collectives, local(): lax.all_to_all(row_buffer, 'store', split_axis=0, concat_axis=0, tiled=True)  39.4 us
    all_to_all x3, blocking collectives, local(): lax.all_to_all(outer, 'store', split_axis=0, concat_axis=0, tiled=True)  39.4 us
    all_gather x1, waiting for transfers between devices, local(): lax.all_gather(flattened_down, 'store', axis=0, tiled=True)  21.9 us
    all_gather x1, waiting for transfers between devices, local(): lax.all_gather(flattened_up, 'store', axis=0, tiled=True)  20.9 us
    dot_general x4, matrix products, local(): jnp.dot(normed, base_projection_weight, preferred_element_type=jnp.float32)  20.1 us
  transfers between devices with their start and end apart: 13, of which 12 were waited for; matrix products, arithmetic and copies ran while one was open for 4% of the time, Pallas kernels for 0%

commit v1 on v0

v1 whole, which is shorter than its diff:
```python
import functools

import jax
import jax.numpy as jnp
from jax import lax
from jax.experimental import pallas as pl
from jax.experimental.pallas import tpu as pltpu
from jax.sharding import PartitionSpec as P

MESH = pl.DeviceIdType.MESH
STEPS = 4
SCALE = 0.5
EPS = 1e-05
HOPS = (2, 1, 3)
BF = jnp.bfloat16
F32 = jnp.float32


def kernel(
    parts, tok, gain, w, down, up, plan, tgt, slt, out,
    w2, dn, un, acts, ext, sbuf, rbuf, own, xown, state, ids,
    w_send, w_recv, w_loc, a_send, a_recv, a_loc, g_send, g_recv, r_send, r_recv,
):
    rows_all, width = tok.shape
    rows = rows_all // parts
    slots = down.shape[0]
    half = slots // 2
    features = gain.shape[1]
    s = lax.axis_index("store")
    m = lax.axis_index("mp")
    z, c = s // 2, s % 2
    y, x = m // 4, m % 4
    p = x * (1 - c) + y * c
    q = y * (1 - c) + x * c

    def mp_of(pp, qq):
        return (qq * 4 + pp) * (1 - c) + (pp * 4 + qq) * c

    def p_peer(k):
        return (s, mp_of((p + k) % 4, q))

    def q_peer(k):
        return (s, mp_of(p, (q + k) % 4))

    def z_peer(k):
        return (((z + k) % 4) * 2 + c, m)

    mate = (z * 2 + 1 - c, m)

    def remote(src, dst, send, recv, device):
        return pltpu.make_async_remote_copy(
            src_ref=src, dst_ref=dst, send_sem=send, recv_sem=recv,
            device_id=device, device_id_type=MESH,
        )

    barrier = pltpu.get_barrier_semaphore()
    for k in HOPS:
        pl.semaphore_signal(barrier, inc=1, device_id=p_peer(k), device_id_type=MESH)
        pl.semaphore_signal(barrier, inc=1, device_id=q_peer(k), device_id_type=MESH)
    for k in (1, 3):
        pl.semaphore_signal(barrier, inc=1, device_id=z_peer(k), device_id_type=MESH)
    pl.semaphore_signal(barrier, inc=1, device_id=mate, device_id_type=MESH)
    pl.semaphore_wait(barrier, 9)

    lo, hi = pl.ds(0, half), pl.ds(half, half)
    s_left, s_right, s_far = ((z + 3) % 4) * 2 + c, ((z + 1) % 4) * 2 + c, ((z + 2) % 4) * 2 + c

    def adapter_copies(f, src, dst):
        def go(i, a, b, device):
            return remote(a, b, a_send.at[f, i], a_recv.at[f, i], device)

        here = [
            go(0, src.at[lo], dst.at[s, lo], z_peer(1)),
            go(1, src.at[hi], dst.at[s, hi], z_peer(1)),
            go(2, src.at[hi], dst.at[s, hi], z_peer(3)),
            go(3, src.at[lo], dst.at[s, lo], z_peer(3)),
            go(4, src, dst.at[s], mate),
        ]
        on = [
            go(5, dst.at[s_left, lo], dst.at[s_left, lo], z_peer(1)),
            go(6, dst.at[s_right, hi], dst.at[s_right, hi], z_peer(3)),
        ]
        across = [
            go(7 + i, dst.at[o, part], dst.at[o, part], mate)
            for i, (o, part) in enumerate(
                ((s_left, lo), (s_right, hi), (s_left, hi), (s_right, lo), (s_far, lo), (s_far, hi))
            )
        ]
        keep = pltpu.make_async_copy(src, dst.at[s], a_loc.at[f])
        return here, on, across, keep

    d_here, d_on, d_across, d_keep = adapter_copies(0, down, dn)
    u_here, u_on, u_across, u_keep = adapter_copies(1, up, un)

    def begin(here, keep):
        for i in (0, 2, 1, 3, 4):
            here[i].start()
        keep.start()

    begin(d_here, d_keep)

    w_out = []
    for i, k in enumerate(HOPS):
        for j in range(4):
            first = pl.multiple_of(mp_of((p + j) % 4, (q + k) % 4) * width, 128)
            w_out.append(
                remote(
                    w.at[pl.ds(first, width)], w2.at[4 - k, pl.ds(j * width, width)],
                    w_send.at[i, j], w_recv.at[i, j], q_peer(k),
                )
            )
    w_keep = []
    for j in range(4):
        first = pl.multiple_of(mp_of((p + j) % 4, q) * width, 128)
        w_keep.append(
            pltpu.make_async_copy(
                w.at[pl.ds(first, width)], w2.at[0, pl.ds(j * width, width)], w_loc.at[j]
            )
        )

    lane = lax.broadcasted_iota(jnp.int32, (rows, 128), 1)
    low = lane < 64

    def act_copies(h, par):
        return [
            remote(
                acts.at[h, par, :, pl.ds(0, width)],
                acts.at[h, par, :, pl.ds((4 - k) * width, width)],
                g_send.at[h, par, i], g_recv.at[h, par, i], p_peer(k),
            )
            for i, k in enumerate(HOPS)
        ]

    def ext_copies(h, par):
        return [
            remote(
                ext.at[h, par, 0], ext.at[h, par, 4 - k],
                g_send.at[h, par, 3 + i], g_recv.at[h, par, 3 + i], p_peer(k),
            )
            for i, k in enumerate(HOPS)
        ]

    def sum_copies(h, par):
        return [
            remote(
                sbuf.at[h, par, i], rbuf.at[h, par, i],
                r_send.at[h, par, i], r_recv.at[h, par, i], q_peer(k),
            )
            for i, k in enumerate(HOPS)
        ]

    gain_here = gain[:, pl.ds(pl.multiple_of(m * width, 128), width)]

    def send_scaled(h, par):
        now = state[h].astype(F32)
        acts[h, par, :, 0:width] = (now * gain_here).astype(BF)
        for cp in act_copies(h, par):
            cp.start()

    def split(total):
        top = total.astype(BF).astype(F32)
        return top, total - top

    def send_inner(h, par):
        now = state[h].astype(F32)
        square = jnp.sum(now * now, axis=1, keepdims=True)
        mine = acts[h, par, :, 0:width]
        who = ids[h]
        acc = jnp.zeros((rows, 128), F32)
        for g in range(8):
            part = lax.dot_general(
                mine, dn[g], (((1,), (1,)), ((), ())), preferred_element_type=F32
            )
            for t in range(4):
                acc += jnp.where(who == g * 8 + 2 * t, part[:, t * 128:(t + 1) * 128], 0.0)
        acc += pltpu.roll(acc, 64, 1)
        top, rest = split(square)
        ext[h, par, 0] = jnp.where(low, acc, jnp.where(lane == 64, top, rest)).astype(BF)
        for cp in ext_copies(h, par):
            cp.start()

    def multiply(h, par):
        for cp in act_copies(h, par) + ext_copies(h, par):
            cp.wait()
        both = ext[h, par, 0].astype(F32)
        for i in range(1, 4):
            both += ext[h, par, i].astype(F32)
        square = both[:, 64:65] + both[:, 65:66]
        top, rest = split(square)
        extra = jnp.where(low, both, jnp.where(lane == 64, top, rest)).astype(BF)
        xown[h] = jnp.where(low, both, square)
        copies = sum_copies(h, par)
        for i, k in enumerate(HOPS):
            part = jnp.dot(acts[h, par], w2[k], preferred_element_type=F32)
            sbuf[h, par, i, :, 0:width] = part.astype(BF)
            sbuf[h, par, i, :, width:width + 128] = extra
            copies[i].start()
        own[h] = jnp.dot(acts[h, par], w2[0], preferred_element_type=F32)

    def finish(h, par):
        for cp in sum_copies(h, par):
            cp.wait()
        base = own[h]
        both = jnp.zeros((rows, 128), F32)
        for i in range(3):
            base += rbuf[h, par, i, :, 0:width].astype(F32)
            both += rbuf[h, par, i, :, width:width + 128].astype(F32)
        mine = xown[h]
        square = both[:, 64:65] + both[:, 65:66] + mine[:, 64:65]
        scale = lax.rsqrt(square * (1.0 / features) + EPS)
        inner = jnp.where(low, (both + mine) * scale, 0.0)
        inner = (inner + pltpu.roll(inner, 64, 1)).astype(BF).astype(F32)
        who = ids[h]
        outer = jnp.zeros((rows, width), F32)
        for g in range(8):
            spread = jnp.concatenate(
                [jnp.where(who == g * 8 + 2 * t, inner, 0.0).astype(BF) for t in range(4)], axis=1
            )
            outer += jnp.dot(spread, un[g], preferred_element_type=F32)
        delta = (SCALE * outer).astype(BF).astype(F32)
        state[h] = (state[h].astype(F32) + base * scale + delta).astype(BF)

    for h in range(parts):
        state[h] = tok[h * rows:(h + 1) * rows]

    @pl.loop(0, parts)
    def _(h):
        send_scaled(h, 0)

    for j in range(4):
        for i in range(3):
            w_out[i * 4 + j].start()
    for cp in w_keep:
        cp.start()

    for h in range(parts):
        group = jnp.broadcast_to(tgt[h * rows:(h + 1) * rows], (rows, 128))
        place = jnp.broadcast_to(slt[h * rows:(h + 1) * rows], (rows, 128))
        key = group * 4 + place - 8
        chosen = group * 8 + place
        for g in range(8):
            for r in range(4):
                hit = jnp.logical_and(place >= 8, key == g * 4 + r)
                chosen = jnp.where(hit, plan[g, r], chosen)
        ids[h] = chosen - jnp.where(low, 0, 1)

    def pass_on(here, on, across):
        here[0].wait_recv()
        on[0].start()
        across[0].start()
        here[2].wait_recv()
        on[1].start()
        across[1].start()

    def pass_rest(here, across):
        here[1].wait_recv()
        across[2].start()
        here[3].wait_recv()
        across[3].start()

    def pass_last(on, across):
        on[0].wait_recv()
        across[4].start()
        on[1].wait_recv()
        across[5].start()

    def settle(here, on, across, keep):
        here[4].wait_recv()
        keep.wait()
        for cp in across:
            cp.wait_recv()

    def drain(here, on, across):
        for cp in here + on + across:
            cp.wait_send()

    pass_on(d_here, d_on, d_across)
    begin(u_here, u_keep)
    pass_rest(d_here, d_across)
    pass_last(d_on, d_across)
    settle(d_here, d_on, d_across, d_keep)

    @pl.loop(0, parts)
    def _(h):
        send_inner(h, 0)

    pass_on(u_here, u_on, u_across)
    pass_rest(u_here, u_across)
    for cp in w_keep:
        cp.wait()
    for cp in w_out:
        cp.wait()

    def step(t):
        par = t % 2

        @pl.loop(0, parts)
        def _(h):
            multiply(h, par)

        @pl.when(t == 0)
        def _():
            pass_last(u_on, u_across)
            settle(u_here, u_on, u_across, u_keep)

        @pl.loop(0, parts)
        def _(h):
            finish(h, par)

            @pl.when(t < STEPS - 1)
            def _():
                send_scaled(h, 1 - par)
                send_inner(h, 1 - par)

    @pl.loop(0, STEPS)
    def _(t):
        step(t)

    drain(d_here, d_on, d_across)
    drain(u_here, u_on, u_across)
    for h in range(parts):
        out[h * rows:(h + 1) * rows] = state[h]


PARTS = 2


def local(tokens, gain, base_weight, down, up, plan, target, slot):
    rows_all, width = tokens.shape
    owned, rank, _ = down.shape
    stores = 8
    rows = rows_all // PARTS
    dma = pltpu.SemaphoreType.DMA
    vmem = pl.BlockSpec(memory_space=pltpu.VMEM)
    anywhere = pl.BlockSpec(memory_space=pl.ANY)
    return pl.pallas_call(
        functools.partial(kernel, PARTS),
        out_shape=jax.ShapeDtypeStruct((rows_all, width), BF),
        in_specs=[
            vmem, vmem, anywhere, anywhere, anywhere,
            pl.BlockSpec(memory_space=pltpu.SMEM), vmem, vmem,
        ],
        out_specs=vmem,
        scratch_shapes=[
            pltpu.VMEM((4, 4 * width, width), BF),
            pltpu.VMEM((stores, owned * rank, width), BF),
            pltpu.VMEM((stores, owned * rank, width), BF),
            pltpu.VMEM((PARTS, 2, rows, 4 * width), BF),
            pltpu.VMEM((PARTS, 2, 4, rows, 128), BF),
            pltpu.VMEM((PARTS, 2, 3, rows, width + 128), BF),
            pltpu.VMEM((PARTS, 2, 3, rows, width + 128), BF),
            pltpu.VMEM((PARTS, rows, width), F32),
            pltpu.VMEM((PARTS, rows, 128), F32),
            pltpu.VMEM((PARTS, rows, width), BF),
            pltpu.VMEM((PARTS, rows, 128), jnp.int32),
            dma((3, 4)), dma((3, 4)), dma((4,)),
            dma((2, 13)), dma((2, 13)), dma((2,)),
            dma((PARTS, 2, 6)), dma((PARTS, 2, 6)),
            dma((PARTS, 2, 3)), dma((PARTS, 2, 3)),
        ],
        compiler_params=pltpu.CompilerParams(
            collective_id=0, has_side_effects=True, vmem_limit_bytes=56 << 20
        ),
    )(
        tokens, gain.reshape(1, -1), base_weight,
        down.reshape(owned * rank, width), up.reshape(owned * rank, width),
        plan, target, slot.reshape(-1, 1),
    )


def solution(mesh):
    return jax.shard_map(
        local,
        mesh=mesh,
        in_specs=(
            P("store", "mp"),
            P(),
            P(None, "mp"),
            P("store", None, "mp"),
            P("store", None, "mp"),
            P(),
            P("store", None),
            P("store"),
        ),
        out_specs=P("store", "mp"),
        check_vma=False,
    )
```

time: 815 us -> 113 us (0.14)
  waiting for transfers between devices: 520 us -> 0 us
  blocking collectives: 171 us -> 0 us
  Pallas kernels: 0 us -> 107 us
  matrix products: 39.8 us -> 0 us
  local copies, waits for them, and re-layouts: 30.5 us -> 5.89 us
  other arithmetic: 23 us -> 0 us
  starting transfers between devices: 14.8 us -> 0 us
  between operations: 13.8 us -> 0.01 us
    reduce_scatter x4 -> x0, waiting for transfers between devices: 285 us -> none  [local(): lax.psum_scatter(partial_value, 'mp', scatter_dimension=0, tiled=True)]
    all_gather x6 -> x0, waiting for transfers between devices: 223 us -> none  [the longest x4 180 us: local(): whole = lax.all_gather(state, 'mp', axis=1, tiled=True)]
    pallas_call x0 -> x1, Pallas kernels: none -> 107 us  [local(): pl.pallas_call(functools.partial(kernel, PARTS), out_shape=jax.ShapeDtype...]
    all_gather x4 -> x0, blocking collectives: 92.2 us -> none  [local(): inner = lax.all_gather(summed_share, 'mp', axis=0, tiled=True)]
    all_to_all x6 -> x0, blocking collectives: 78.8 us -> none  [the longest x3 39.4 us: local(): lax.all_to_all(row_buffer, 'store', split_axis=0, concat_axis=0, tiled=True)]
    dot_general x14 -> x0, matrix products: 39.8 us -> none  [the longest x4 20.1 us: local(): jnp.dot(normed, base_projection_weight, preferred_element_type=jnp.float32)]
    all_to_all x3 -> x0, starting transfers between devices: 14.3 us -> none  [the longest x1 5.43 us: local(): lax.all_to_all(slot_buffer, 'store', split_axis=0, concat_axis=0, tiled=T...]
    reduce_sum x5 -> x0, other arithmetic: 11.7 us -> none  [the longest x4 11 us: local(): mean_sq = jnp.mean(values * values, axis=1, keepdims=True)]
  transfers between devices with their start and end apart: 13 -> 0, of which waited for: 12 -> 0; matrix products, arithmetic and copies ran while one was open for 4% -> 0% of each run, Pallas kernels for 0% -> 0%
where the time goes in v1:
time: 113 us
  Pallas kernels  107 us (95%)
  local copies, waits for them, and re-layouts  5.89 us (5%)
    pallas_call x1, Pallas kernels, local(): pl.pallas_call(functools.partial(kernel, PARTS), out_shape=jax.ShapeDtype...  107 us
    unnamed x3, local copies, waits for them, and re-layouts  4.44 us

profile of v1, /device:TPU:0, one launch (start us, length us, event | category | flops | bytes accessed | tf_op | source)
XLA Modules:
  0.0 112.5 jit_solution(15720052895065354463)
XLA Ops:
  0.0 1.3 %copy.11.plan = s32[8,4]{1,0:T(8,128)} copy(s32[8,4]{0,1:T(4,128)} %param.13) | data formatting | bytes 256 | tf_op args[5]
  1.3 1.5 %copy.12.tgt = s32[256,1]{1,0:T(8,128)} copy(s32[256,1]{0,1:T(1,128)} %param.14) | data formatting | bytes 2048 | tf_op args[6]
  2.8 1.5 %copy.13.slt = s32[256,1]{1,0:T(8,128)} copy(s32[256,1]{0,1:T(1,128)} %bitcast.7) | data formatting | bytes 2048 | tf_op jit(solution)/shard_map/reshape | solution.py:367
  4.3 106.6 %shard_map.82 = bf16[256,384]{1,0:T(8,128)(2,1)} custom-call(bf16[256,384]{1,0:T(8,128)(2,1)} %tok.1, f32[1,6144]{1,0:T(1,128)} %bitcast.6, bf16[6144,384]{1,0:T(8,128)(2,1)} %w.1, bf16[512,384]{1,0:T(8,128)(2,1)} %bitcast.4, bf16[512,384]{1,0:T(8,128)(2,1)} %bitcast.5, s32[8,4]{1,0:T(8,128)} %copy.11.plan, s32[256,1]{1,0:T(8,128)} %copy.12.tgt, ...), custom_call_target="tpu_custom_call" | custom-call | tf_op jit(solution)/shard_map/pallas_call | solution.py:336
  110.9 1.6 %copy.15 = bf16[256,384]{1,0:T(8,128)(2,1)} copy(bf16[256,384]{1,0:T(8,128)(2,1)} %shard_map.82) | data formatting | bytes 393216

commit v2 on v1

v2 whole, which is shorter than its diff:
```python
import functools

import jax
import jax.numpy as jnp
from jax import lax
from jax.experimental import pallas as pl
from jax.experimental.pallas import tpu as pltpu
from jax.sharding import PartitionSpec as P

MESH = pl.DeviceIdType.MESH
STEPS = 4
SCALE = 0.5
EPS = 1e-05
HOPS = (1, 3, 2)
PLACE = {1: 0, 3: 1, 2: 2, 0: 3}
BF = jnp.bfloat16
F32 = jnp.float32


def kernel(
    parts, groups, tok, gain, w, down, up, plan, tgt, slt, out,
    w2, dn, un, acts, ext, sbuf, rbuf, xbuf, xrec, own, xown, sown, delta, scale, state, ids,
    w_send, w_recv, w_loc, a_send, a_recv, a_loc,
    g_send, g_recv, e_send, e_recv, r_send, r_recv, x_send, x_recv,
):
    rows_all, width = tok.shape
    rows = rows_all // parts
    block = rows_all // groups
    deep = block // 2
    slots = down.shape[0]
    half = slots // 2
    features = gain.shape[1]
    s = lax.axis_index("store")
    m = lax.axis_index("mp")
    z, c = s // 2, s % 2
    y, x = m // 4, m % 4
    p = x * (1 - c) + y * c
    q = y * (1 - c) + x * c

    def mp_of(pp, qq):
        return (qq * 4 + pp) * (1 - c) + (pp * 4 + qq) * c

    def p_peer(k):
        return (s, mp_of((p + k) % 4, q))

    def q_peer(k):
        return (s, mp_of(p, (q + k) % 4))

    def z_peer(k):
        return (((z + k) % 4) * 2 + c, m)

    mate = (z * 2 + 1 - c, m)

    def remote(src, dst, send, recv, device):
        return pltpu.make_async_remote_copy(
            src_ref=src, dst_ref=dst, send_sem=send, recv_sem=recv,
            device_id=device, device_id_type=MESH,
        )

    barrier = pltpu.get_barrier_semaphore()
    for k in HOPS:
        pl.semaphore_signal(barrier, inc=1, device_id=p_peer(k), device_id_type=MESH)
        pl.semaphore_signal(barrier, inc=1, device_id=q_peer(k), device_id_type=MESH)
    for k in (1, 3):
        pl.semaphore_signal(barrier, inc=1, device_id=z_peer(k), device_id_type=MESH)
    pl.semaphore_signal(barrier, inc=1, device_id=mate, device_id_type=MESH)
    pl.semaphore_wait(barrier, 9)

    lo, hi = pl.ds(0, half), pl.ds(half, half)
    s_left, s_right, s_far = ((z + 3) % 4) * 2 + c, ((z + 1) % 4) * 2 + c, ((z + 2) % 4) * 2 + c

    def adapter_copies(f, src, dst):
        def go(i, a, b, device):
            return remote(a, b, a_send.at[f, i], a_recv.at[f, i], device)

        here = [
            go(0, src.at[lo], dst.at[s, lo], z_peer(1)),
            go(1, src.at[hi], dst.at[s, hi], z_peer(1)),
            go(2, src.at[hi], dst.at[s, hi], z_peer(3)),
            go(3, src.at[lo], dst.at[s, lo], z_peer(3)),
            go(4, src, dst.at[s], mate),
        ]
        on = [
            go(5, dst.at[s_left, lo], dst.at[s_left, lo], z_peer(1)),
            go(6, dst.at[s_right, hi], dst.at[s_right, hi], z_peer(3)),
        ]
        across = [
            go(7 + i, dst.at[o, part], dst.at[o, part], mate)
            for i, (o, part) in enumerate(
                ((s_left, lo), (s_right, hi), (s_left, hi), (s_right, lo), (s_far, lo), (s_far, hi))
            )
        ]
        keep = pltpu.make_async_copy(src, dst.at[s], a_loc.at[f])
        return here, on, across, keep

    d_here, d_on, d_across, d_keep = adapter_copies(0, down, dn)
    u_here, u_on, u_across, u_keep = adapter_copies(1, up, un)

    def begin(here, keep):
        for i in (0, 2, 1, 3, 4):
            here[i].start()
        keep.start()

    begin(d_here, d_keep)

    w_out = []
    for i, k in enumerate(HOPS):
        for j in range(4):
            first = pl.multiple_of(mp_of((p + j) % 4, (q + k) % 4) * width, 128)
            w_out.append(
                remote(
                    w.at[pl.ds(first, width)],
                    w2.at[pl.ds(j * width, width), pl.ds(PLACE[4 - k] * width, width)],
                    w_send.at[i, j], w_recv.at[i, j], q_peer(k),
                )
            )
    w_keep = []
    for j in range(4):
        first = pl.multiple_of(mp_of((p + j) % 4, q) * width, 128)
        w_keep.append(
            pltpu.make_async_copy(
                w.at[pl.ds(first, width)],
                w2.at[pl.ds(j * width, width), pl.ds(PLACE[0] * width, width)],
                w_loc.at[j],
            )
        )

    low = lax.broadcasted_iota(jnp.int32, (deep, 128), 1) < 64
    diagonal = lax.broadcasted_iota(jnp.int32, (block, 128), 0) == lax.broadcasted_iota(
        jnp.int32, (block, 128), 1
    )
    line = lax.broadcasted_iota(jnp.int32, (16, 128), 0)

    def part(h):
        return pl.ds(pl.multiple_of(h * rows, rows), rows)

    def group(g):
        return pl.ds(pl.multiple_of(g * block, block), block)

    def act_copies(h, par):
        return [
            remote(
                acts.at[par, part(h), pl.ds(0, width)],
                acts.at[par, part(h), pl.ds((4 - k) * width, width)],
                g_send.at[par, h, i], g_recv.at[par, h, i], p_peer(k),
            )
            for i, k in enumerate(HOPS)
        ]

    def ext_copies(g, par):
        return [
            remote(
                ext.at[par, g, 0], ext.at[par, g, 4 - k],
                e_send.at[par, g, i], e_recv.at[par, g, i], p_peer(k),
            )
            for i, k in enumerate(HOPS)
        ]

    def sum_copies(h, par):
        return [
            remote(
                sbuf.at[par, i, part(h)], rbuf.at[par, i, part(h)],
                r_send.at[par, h, i], r_recv.at[par, h, i], q_peer(k),
            )
            for i, k in enumerate(HOPS)
        ]

    def inner_copies(g, par):
        return [
            remote(
                xbuf.at[par, g], xrec.at[par, g, i],
                x_send.at[par, g, i], x_recv.at[par, g, i], q_peer(k),
            )
            for i, k in enumerate(HOPS)
        ]

    gain_here = gain[:, pl.ds(pl.multiple_of(m * width, 128), width)]

    def send_scaled(h, par):
        acts[par, part(h), 0:width] = (state[part(h)].astype(F32) * gain_here).astype(BF)
        for cp in act_copies(h, par):
            cp.start()

    def as_column(row):
        return jnp.sum(jnp.where(diagonal, row, 0.0), axis=1, keepdims=True)

    def packed(inner, square):
        top = square.astype(BF).astype(F32)
        tail = jnp.where(line == 0, top, jnp.where(line == 1, square - top, 0.0))
        return inner.astype(BF), tail.astype(BF)

    def send_inner(g, par):
        now = state[group(g)].astype(F32)
        square = jnp.sum(now * now, axis=1, keepdims=True)
        square = jnp.sum(jnp.where(diagonal, square, 0.0), axis=0, keepdims=True)
        mine = acts[par, group(g), 0:width]
        who = ids[group(g)]
        acc = jnp.zeros((block, 128), F32)
        for a in range(8):
            value = lax.dot_general(
                mine, dn[a], (((1,), (1,)), ((), ())), preferred_element_type=F32
            )
            for t in range(4):
                acc += jnp.where(
                    who == float(a * 8 + 2 * t), value[:, t * 128:(t + 1) * 128], 0.0
                )
        acc += pltpu.roll(acc, 64, 1)
        body, tail = packed(jnp.where(low, acc[:deep], acc[deep:]), square)
        ext[par, g, 0, 0:deep] = body
        ext[par, g, 0, deep:deep + 16] = tail
        for cp in ext_copies(g, par):
            cp.start()

    def multiply(h, par):
        for cp in act_copies(h, par):
            cp.wait()
        copies = sum_copies(h, par)
        left = acts[par, part(h)]
        value = jnp.dot(left, w2[:, 0:2 * width], preferred_element_type=F32).astype(BF)
        sbuf[par, 0, part(h)] = value[:, :width]
        copies[0].start()
        sbuf[par, 1, part(h)] = value[:, width:]
        copies[1].start()
        value = jnp.dot(left, w2[:, 2 * width:4 * width], preferred_element_type=F32)
        sbuf[par, 2, part(h)] = value[:, :width].astype(BF)
        copies[2].start()
        own[part(h)] = value[:, width:]

    def forward(g, par):
        for cp in ext_copies(g, par):
            cp.wait()
        both = ext[par, g, 0].astype(F32)
        for i in range(1, 4):
            both += ext[par, g, i].astype(F32)
        inner, square = both[:deep], both[deep:deep + 1] + both[deep + 1:deep + 2]
        body, tail = packed(inner, square)
        xbuf[par, g, 0:deep] = body
        xbuf[par, g, deep:deep + 16] = tail
        for cp in inner_copies(g, par):
            cp.start()
        xown[g] = inner
        sown[g] = jnp.broadcast_to(square, (8, 128))

    def adapt(g, par):
        for cp in inner_copies(g, par):
            cp.wait()
        both = xrec[par, g, 0].astype(F32)
        for i in range(1, 3):
            both += xrec[par, g, i].astype(F32)
        square = both[deep:deep + 1] + both[deep + 1:deep + 2] + sown[g, 0:1]
        factor = as_column(lax.rsqrt(square * (1.0 / features) + EPS))
        scale[group(g)] = jnp.broadcast_to(factor, (block, 128))
        inner = both[:deep] + xown[g]
        other = pltpu.roll(inner, 64, 1)
        inner = jnp.concatenate([jnp.where(low, inner, other), jnp.where(low, other, inner)], 0)
        inner = (inner * factor).astype(BF).astype(F32)
        who = ids[group(g)]
        outer = jnp.zeros((block, width), F32)
        for a in range(8):
            spread = jnp.concatenate(
                [
                    jnp.where(who == float(a * 8 + 2 * t), inner, 0.0).astype(BF)
                    for t in range(4)
                ],
                axis=1,
            )
            outer += jnp.dot(spread, un[a], preferred_element_type=F32)
        delta[group(g)] = (SCALE * outer).astype(BF)

    def finish(h, par):
        for cp in sum_copies(h, par):
            cp.wait()
        base = own[part(h)]
        for i in range(3):
            base += rbuf[par, i, part(h)].astype(F32)
        factor = jnp.concatenate([scale[part(h)]] * (width // 128), axis=1)
        now = state[part(h)].astype(F32) + base * factor + delta[part(h)].astype(F32)
        state[part(h)] = now.astype(BF)

    state[...] = tok[...]

    @pl.loop(0, parts)
    def _(h):
        send_scaled(h, 0)

    for j in range(4):
        for i in range(3):
            w_out[i * 4 + j].start()
    for cp in w_keep:
        cp.start()

    wanted = tgt[...]
    place = slt[...]
    key = wanted * 4 + place - 8
    chosen = wanted * 8 + place
    for a in range(8):
        for r in range(4):
            hit = jnp.logical_and(place >= 8, key == a * 4 + r)
            chosen = jnp.where(hit, plan[r, a], chosen)
    chosen = chosen.astype(F32)
    upper = (lax.broadcasted_iota(jnp.int32, (block, 128), 1) >= 64).astype(F32)
    for g in range(groups):
        ids[g * block:(g + 1) * block] = as_column(chosen[:, g * block:(g + 1) * block]) - upper

    def pass_on(here, on, across):
        here[0].wait_recv()
        on[0].start()
        across[0].start()
        here[2].wait_recv()
        on[1].start()
        across[1].start()

    def pass_rest(here, across):
        here[1].wait_recv()
        across[2].start()
        here[3].wait_recv()
        across[3].start()

    def pass_last(on, across):
        on[0].wait_recv()
        across[4].start()
        on[1].wait_recv()
        across[5].start()

    def settle(here, across, keep):
        here[4].wait_recv()
        keep.wait()
        for cp in across:
            cp.wait_recv()

    def drain(here, on, across):
        for cp in here + on + across:
            cp.wait_send()

    pass_on(d_here, d_on, d_across)
    begin(u_here, u_keep)
    pass_rest(d_here, d_across)
    pass_last(d_on, d_across)
    settle(d_here, d_across, d_keep)

    @pl.loop(0, groups)
    def _(g):
        send_inner(g, 0)

    pass_on(u_here, u_on, u_across)
    pass_rest(u_here, u_across)
    for cp in w_keep:
        cp.wait()
    for cp in w_out:
        cp.wait()

    per = parts // groups

    @pl.loop(0, STEPS)
    def _(t):
        par = t % 2

        @pl.loop(0, groups)
        def _(g):
            multiply(g * per, par)
            forward(g, par)
            for i in range(1, per):
                multiply(g * per + i, par)

        @pl.when(t == 0)
        def _():
            pass_last(u_on, u_across)
            settle(u_here, u_across, u_keep)

        @pl.loop(0, groups)
        def _(g):
            adapt(g, par)

            @pl.loop(0, per)
            def _(i):
                h = g * per + i
                finish(h, par)

                @pl.when(t < STEPS - 1)
                def _():
                    send_scaled(h, 1 - par)

            @pl.when(t < STEPS - 1)
            def _():
                send_inner(g, 1 - par)

    drain(d_here, d_on, d_across)
    drain(u_here, u_on, u_across)
    out[...] = state[...]


PARTS = 4
GROUPS = 2


def local(tokens, gain, base_weight, down, up, plan, target, slot):
    rows_all, width = tokens.shape
    owned, rank, _ = down.shape
    stores = 8
    lines = rows_all // GROUPS // 2 + 16
    dma = pltpu.SemaphoreType.DMA
    vmem = pl.BlockSpec(memory_space=pltpu.VMEM)
    anywhere = pl.BlockSpec(memory_space=pl.ANY)
    return pl.pallas_call(
        functools.partial(kernel, PARTS, GROUPS),
        out_shape=jax.ShapeDtypeStruct((rows_all, width), BF),
        in_specs=[
            vmem, vmem, anywhere, anywhere, anywhere,
            pl.BlockSpec(memory_space=pltpu.SMEM), vmem, vmem,
        ],
        out_specs=vmem,
        scratch_shapes=[
            pltpu.VMEM((4 * width, 4 * width), BF),
            pltpu.VMEM((stores, owned * rank, width), BF),
            pltpu.VMEM((stores, owned * rank, width), BF),
            pltpu.VMEM((2, rows_all, 4 * width), BF),
            pltpu.VMEM((2, GROUPS, 4, lines, 128), BF),
            pltpu.VMEM((2, 3, rows_all, width), BF),
            pltpu.VMEM((2, 3, rows_all, width), BF),
            pltpu.VMEM((2, GROUPS, lines, 128), BF),
            pltpu.VMEM((2, GROUPS, 3, lines, 128), BF),
            pltpu.VMEM((rows_all, width), F32),
            pltpu.VMEM((GROUPS, lines - 16, 128), F32),
            pltpu.VMEM((GROUPS, 8, 128), F32),
            pltpu.VMEM((rows_all, width), BF),
            pltpu.VMEM((rows_all, 128), F32),
            pltpu.VMEM((rows_all, width), BF),
            pltpu.VMEM((rows_all, 128), F32),
            dma((3, 4)), dma((3, 4)), dma((4,)),
            dma((2, 13)), dma((2, 13)), dma((2,)),
            dma((2, PARTS, 3)), dma((2, PARTS, 3)),
            dma((2, GROUPS, 3)), dma((2, GROUPS, 3)),
            dma((2, PARTS, 3)), dma((2, PARTS, 3)),
            dma((2, GROUPS, 3)), dma((2, GROUPS, 3)),
        ],
        compiler_params=pltpu.CompilerParams(
            collective_id=0, has_side_effects=True, vmem_limit_bytes=56 << 20
        ),
    )(
        tokens, gain.reshape(1, -1), base_weight,
        down.reshape(owned * rank, width), up.reshape(owned * rank, width),
        plan.T, target.reshape(1, -1), slot.reshape(1, -1),
    )


def solution(mesh):
    return jax.shard_map(
        local,
        mesh=mesh,
        in_specs=(
            P("store", "mp"),
            P(),
            P(None, "mp"),
            P("store", None, "mp"),
            P("store", None, "mp"),
            P(),
            P("store", None),
            P("store"),
        ),
        out_specs=P("store", "mp"),
        check_vma=False,
    )
```

time: 113 us -> 95.9 us (0.85)
  Pallas kernels: 107 us -> 93.5 us
  local copies, waits for them, and re-layouts: 5.89 us -> 1.62 us
    pallas_call x1, Pallas kernels: 107 us -> 93.5 us  [local(): pl.pallas_call(functools.partial(kernel, PARTS, GROUPS), out_shape=jax.Sh...]
    unnamed x3 -> x1, local copies, waits for them, and re-layouts: 4.44 us -> 1.62 us
    reshape x1 -> x0, local copies, waits for them, and re-layouts: 1.45 us -> none  [local(): slot.reshape(-1, 1)]
where the time goes in v2:
time: 95.9 us; the launch traced here: 95.2 us
  Pallas kernels  93.5 us (97%)
  local copies, waits for them, and re-layouts  1.62 us (2%)
    pallas_call x1, Pallas kernels, local(): pl.pallas_call(functools.partial(kernel, PARTS, GROUPS), out_shape=jax.Sh...  93.5 us

profile of v2, /device:TPU:0, one launch (start us, length us, event | category | flops | bytes accessed | tf_op | source)
XLA Modules:
  0.0 95.2 jit_solution(9670890045481341463)
XLA Ops:
  0.0 93.5 %shard_map.82 = bf16[256,384]{1,0:T(8,128)(2,1)} custom-call(bf16[256,384]{1,0:T(8,128)(2,1)} %tok.1, f32[1,6144]{1,0:T(1,128)} %bitcast.8, bf16[6144,384]{1,0:T(8,128)(2,1)} %w.1, bf16[512,384]{1,0:T(8,128)(2,1)} %bitcast.6, bf16[512,384]{1,0:T(8,128)(2,1)} %bitcast.7, s32[4,8]{1,0:T(4,128)} %bitcast.9, s32[1,256]{1,0:T(1,128)} %bitcast.10, s32[1,256]{1,0:T(1,128)} %bitcast.11), custom_call_target="tpu_custom_call" | custom-call | tf_op jit(solution)/shard_map/pallas_call | solution.py:404
  93.5 1.6 %copy.10 = bf16[256,384]{1,0:T(8,128)(2,1)} copy(bf16[256,384]{1,0:T(8,128)(2,1)} %shard_map.82) | data formatting | bytes 393216

commit v3 on v2

--- a/solution.py
+++ b/solution.py
@@ -21,7 +21,7 @@
     parts, groups, tok, gain, w, down, up, plan, tgt, slt, out,
     w2, dn, un, acts, ext, sbuf, rbuf, xbuf, xrec, own, xown, sown, delta, scale, state, ids,
     w_send, w_recv, w_loc, a_send, a_recv, a_loc,
-    g_send, g_recv, e_send, e_recv, r_send, r_recv, x_send, x_recv,
+    g_send, g_recv, e_send, e_recv, r_send, r_recv, x_send, x_recv, pair,
 ):
     rows_all, width = tok.shape
     rows = rows_all // parts
@@ -354,6 +354,8 @@
     @pl.loop(0, STEPS)
     def _(t):
         par = t % 2
+        pl.semaphore_signal(pair, inc=1, device_id=mate, device_id_type=MESH)
+        pl.semaphore_wait(pair, 1)
 
         @pl.loop(0, groups)
         def _(g):
@@ -432,6 +434,7 @@
             dma((2, GROUPS, 3)), dma((2, GROUPS, 3)),
             dma((2, PARTS, 3)), dma((2, PARTS, 3)),
             dma((2, GROUPS, 3)), dma((2, GROUPS, 3)),
+            pltpu.SemaphoreType.REGULAR,
         ],
         compiler_params=pltpu.CompilerParams(
             collective_id=0, has_side_effects=True, vmem_limit_bytes=56 << 20

time: 95.9 us -> 90.6 us (0.945)
  Pallas kernels: 93.5 us -> 88.2 us
    pallas_call x1, Pallas kernels: 93.5 us -> 88.2 us  [local(): pl.pallas_call(functools.partial(kernel, PARTS, GROUPS), out_shape=jax.Sh...]
where the time goes in v3:
time: 90.6 us; the launch traced here: 89.8 us
  Pallas kernels  88.2 us (97%)
  local copies, waits for them, and re-layouts  1.62 us (2%)
    pallas_call x1, Pallas kernels, local(): pl.pallas_call(functools.partial(kernel, PARTS, GROUPS), out_shape=jax.Sh...  88.2 us

profile of v3, /device:TPU:0, one launch (start us, length us, event | category | flops | bytes accessed | tf_op | source)
XLA Modules:
  0.0 89.8 jit_solution(3841903059472476567)
XLA Ops:
  0.0 88.2 %shard_map.82 = bf16[256,384]{1,0:T(8,128)(2,1)} custom-call(bf16[256,384]{1,0:T(8,128)(2,1)} %tok.1, f32[1,6144]{1,0:T(1,128)} %bitcast.8, bf16[6144,384]{1,0:T(8,128)(2,1)} %w.1, bf16[512,384]{1,0:T(8,128)(2,1)} %bitcast.6, bf16[512,384]{1,0:T(8,128)(2,1)} %bitcast.7, s32[4,8]{1,0:T(4,128)} %bitcast.9, s32[1,256]{1,0:T(1,128)} %bitcast.10, s32[1,256]{1,0:T(1,128)} %bitcast.11), custom_call_target="tpu_custom_call" | custom-call | tf_op jit(solution)/shard_map/pallas_call | solution.py:406
  88.2 1.6 %copy.10 = bf16[256,384]{1,0:T(8,128)(2,1)} copy(bf16[256,384]{1,0:T(8,128)(2,1)} %shard_map.82) | data formatting | bytes 393216

commit v4 on v3

--- a/solution.py
+++ b/solution.py
@@ -11,15 +11,16 @@
 STEPS = 4
 SCALE = 0.5
 EPS = 1e-05
-HOPS = (1, 3, 2)
-PLACE = {1: 0, 3: 1, 2: 2, 0: 3}
+HOPS = (2, 1, 3)
+PLACE = {2: 0, 0: 1, 1: 2, 3: 3}
 BF = jnp.bfloat16
 F32 = jnp.float32
 
 
 def kernel(
     parts, groups, tok, gain, w, down, up, plan, tgt, slt, out,
-    w2, dn, un, acts, ext, sbuf, rbuf, xbuf, xrec, own, xown, sown, delta, scale, state, ids,
+    w2, dn, un, acts, ext, sbuf, rbuf, xbuf, xrec, own, early, xown, sown, delta, scale, state, ids,
+    gbuf, tbuf, sbuf_slot, i_sem, o_sem,
     w_send, w_recv, w_loc, a_send, a_recv, a_loc,
     g_send, g_recv, e_send, e_recv, r_send, r_recv, x_send, x_recv, pair,
 ):
@@ -57,6 +58,17 @@
             device_id=device, device_id_type=MESH,
         )
 
+    inputs = [
+        pltpu.make_async_copy(tok, state, i_sem.at[0]),
+        pltpu.make_async_copy(
+            gain.at[:, pl.ds(pl.multiple_of(m * width, 128), width)], gbuf, i_sem.at[1]
+        ),
+        pltpu.make_async_copy(tgt, tbuf, i_sem.at[2]),
+        pltpu.make_async_copy(slt, sbuf_slot, i_sem.at[3]),
+    ]
+    for cp in inputs:
+        cp.start()
+
     barrier = pltpu.get_barrier_semaphore()
     for k in HOPS:
         pl.semaphore_signal(barrier, inc=1, device_id=p_peer(k), device_id_type=MESH)
@@ -174,10 +186,9 @@
             for i, k in enumerate(HOPS)
         ]
 
-    gain_here = gain[:, pl.ds(pl.multiple_of(m * width, 128), width)]
 
     def send_scaled(h, par):
-        acts[par, part(h), 0:width] = (state[part(h)].astype(F32) * gain_here).astype(BF)
+        acts[par, part(h), 0:width] = (state[part(h)].astype(F32) * gbuf[...]).astype(BF)
         for cp in act_copies(h, par):
             cp.start()
 
@@ -211,20 +222,41 @@
         for cp in ext_copies(g, par):
             cp.start()
 
-    def multiply(h, par):
+    def arrive(h, par):
         for cp in act_copies(h, par):
             cp.wait()
+
+    def far(h, par):
+        value = jnp.dot(acts[par, part(h)], w2[:, 0:2 * width], preferred_element_type=F32)
+        sbuf[par, 0, part(h)] = value[:, :width].astype(BF)
+        sum_copies(h, par)[0].start()
+        own[part(h)] = value[:, width:]
+
+    def send_near(h, par, value):
         copies = sum_copies(h, par)
-        left = acts[par, part(h)]
-        value = jnp.dot(left, w2[:, 0:2 * width], preferred_element_type=F32).astype(BF)
-        sbuf[par, 0, part(h)] = value[:, :width]
-        copies[0].start()
-        sbuf[par, 1, part(h)] = value[:, width:]
+        value = value.astype(BF)
+        sbuf[par, 1, part(h)] = value[:, :width]
         copies[1].start()
-        value = jnp.dot(left, w2[:, 2 * width:4 * width], preferred_element_type=F32)
-        sbuf[par, 2, part(h)] = value[:, :width].astype(BF)
+        sbuf[par, 2, part(h)] = value[:, width:]
         copies[2].start()
-        own[part(h)] = value[:, width:]
+
+    def multiply(h, par, first):
+        @pl.when(jnp.logical_not(first))
+        def _():
+            arrive(h, par)
+            far(h, par)
+            send_near(
+                h, par,
+                jnp.dot(acts[par, part(h)], w2[:, 2 * width:], preferred_element_type=F32),
+            )
+
+        @pl.when(first)
+        def _():
+            last = jnp.dot(
+                acts[par, part(h), 3 * width:], w2[3 * width:, 2 * width:],
+                preferred_element_type=F32,
+            )
+            send_near(h, par, early[part(h)] + last)
 
     def forward(g, par):
         for cp in ext_copies(g, par):
@@ -277,20 +309,28 @@
         now = state[part(h)].astype(F32) + base * factor + delta[part(h)].astype(F32)
         state[part(h)] = now.astype(BF)
 
-    state[...] = tok[...]
+    def result(h):
+        return pltpu.make_async_copy(state.at[part(h)], out.at[part(h)], o_sem.at[h])
+
+    inputs[0].wait()
+    inputs[1].wait()
 
     @pl.loop(0, parts)
     def _(h):
         send_scaled(h, 0)
 
     for j in range(4):
-        for i in range(3):
+        w_out[j].start()
+    for j in range(4):
+        for i in (1, 2):
             w_out[i * 4 + j].start()
     for cp in w_keep:
         cp.start()
 
-    wanted = tgt[...]
-    place = slt[...]
+    inputs[2].wait()
+    inputs[3].wait()
+    wanted = tbuf[...]
+    place = sbuf_slot[...]
     key = wanted * 4 + place - 8
     chosen = wanted * 8 + place
     for a in range(8):
@@ -344,10 +384,32 @@
 
     pass_on(u_here, u_on, u_across)
     pass_rest(u_here, u_across)
-    for cp in w_keep:
+    for cp in w_keep + w_out[:4]:
         cp.wait()
-    for cp in w_out:
-        cp.wait()
+
+    @pl.loop(0, parts)
+    def _(h):
+        arrive(h, 0)
+        far(h, 0)
+
+    @pl.loop(0, groups)
+    def _(g):
+        forward(g, 0)
+
+    pass_last(u_on, u_across)
+    for j in range(3):
+        w_out[4 + j].wait()
+        w_out[8 + j].wait()
+
+    @pl.loop(0, parts)
+    def _(h):
+        early[part(h)] = jnp.dot(
+            acts[0, part(h), 0:3 * width], w2[0:3 * width, 2 * width:],
+            preferred_element_type=F32,
+        )
+
+    w_out[7].wait()
+    w_out[11].wait()
 
     per = parts // groups
 
@@ -359,14 +421,17 @@
 
         @pl.loop(0, groups)
         def _(g):
-            multiply(g * per, par)
-            forward(g, par)
+            multiply(g * per, par, t == 0)
+
+            @pl.when(t > 0)
+            def _():
+                forward(g, par)
+
             for i in range(1, per):
-                multiply(g * per + i, par)
+                multiply(g * per + i, par, t == 0)
 
         @pl.when(t == 0)
         def _():
-            pass_last(u_on, u_across)
             settle(u_here, u_across, u_keep)
 
         @pl.loop(0, groups)
@@ -382,13 +447,18 @@
                 def _():
                     send_scaled(h, 1 - par)
 
+                @pl.when(t == STEPS - 1)
+                def _():
+                    result(h).start()
+
             @pl.when(t < STEPS - 1)
             def _():
                 send_inner(g, 1 - par)
 
     drain(d_here, d_on, d_across)
     drain(u_here, u_on, u_across)
-    out[...] = state[...]
+    for h in range(parts):
+        result(h).wait()
 
 
 PARTS = 4
@@ -401,16 +471,15 @@
     stores = 8
     lines = rows_all // GROUPS // 2 + 16
     dma = pltpu.SemaphoreType.DMA
-    vmem = pl.BlockSpec(memory_space=pltpu.VMEM)
     anywhere = pl.BlockSpec(memory_space=pl.ANY)
     return pl.pallas_call(
         functools.partial(kernel, PARTS, GROUPS),
         out_shape=jax.ShapeDtypeStruct((rows_all, width), BF),
         in_specs=[
-            vmem, vmem, anywhere, anywhere, anywhere,
-            pl.BlockSpec(memory_space=pltpu.SMEM), vmem, vmem,
+            anywhere, anywhere, anywhere, anywhere, anywhere,
+            pl.BlockSpec(memory_space=pltpu.SMEM), anywhere, anywhere,
         ],
-        out_specs=vmem,
+        out_specs=anywhere,
         scratch_shapes=[
             pltpu.VMEM((4 * width, 4 * width), BF),
             pltpu.VMEM((stores, owned * rank, width), BF),
@@ -422,12 +491,17 @@
             pltpu.VMEM((2, GROUPS, lines, 128), BF),
             pltpu.VMEM((2, GROUPS, 3, lines, 128), BF),
             pltpu.VMEM((rows_all, width), F32),
+            pltpu.VMEM((rows_all, 2 * width), F32),
             pltpu.VMEM((GROUPS, lines - 16, 128), F32),
             pltpu.VMEM((GROUPS, 8, 128), F32),
             pltpu.VMEM((rows_all, width), BF),
             pltpu.VMEM((rows_all, 128), F32),
             pltpu.VMEM((rows_all, width), BF),
             pltpu.VMEM((rows_all, 128), F32),
+            pltpu.VMEM((1, width), F32),
+            pltpu.VMEM((1, rows_all), jnp.int32),
+            pltpu.VMEM((1, rows_all), jnp.int32),
+            dma((4,)), dma((PARTS,)),
             dma((3, 4)), dma((3, 4)), dma((4,)),
             dma((2, 13)), dma((2, 13)), dma((2,)),
             dma((2, PARTS, 3)), dma((2, PARTS, 3)),

time: 90.6 us -> 85.9 us (0.948)
  Pallas kernels: 88.2 us -> 83.1 us
    pallas_call x1, Pallas kernels: 88.2 us -> 83.1 us  [local(): pl.pallas_call(functools.partial(kernel, PARTS, GROUPS), out_shape=jax.Sh...]
where the time goes in v4:
time: 85.9 us; the launch traced here: 84.7 us
  Pallas kernels  83.1 us (97%)
  local copies, waits for them, and re-layouts  1.62 us (2%)
    pallas_call x1, Pallas kernels, local(): pl.pallas_call(functools.partial(kernel, PARTS, GROUPS), out_shape=jax.Sh...  83.1 us

profile of v4, /device:TPU:0, one launch (start us, length us, event | category | flops | bytes accessed | tf_op | source)
XLA Modules:
  0.0 84.7 jit_solution(12538091696618261636)
XLA Ops:
  0.0 83.1 %shard_map.82 = bf16[256,384]{1,0:T(8,128)(2,1)} custom-call(bf16[256,384]{1,0:T(8,128)(2,1)} %tok.1, f32[1,6144]{1,0:T(1,128)} %bitcast.8, bf16[6144,384]{1,0:T(8,128)(2,1)} %w.1, bf16[512,384]{1,0:T(8,128)(2,1)} %bitcast.6, bf16[512,384]{1,0:T(8,128)(2,1)} %bitcast.7, s32[4,8]{1,0:T(4,128)} %bitcast.9, s32[1,256]{1,0:T(1,128)} %bitcast.10, s32[1,256]{1,0:T(1,128)} %bitcast.11), custom_call_target="tpu_custom_call" | custom-call | tf_op jit(solution)/shard_map/pallas_call | solution.py:475
  83.1 1.6 %copy.10 = bf16[256,384]{1,0:T(8,128)(2,1)} copy(bf16[256,384]{1,0:T(8,128)(2,1)} %shard_map.82) | data formatting | bytes 393216

commit v5 on v4

--- a/solution.py
+++ b/solution.py
@@ -20,7 +20,7 @@
 def kernel(
     parts, groups, tok, gain, w, down, up, plan, tgt, slt, out,
     w2, dn, un, acts, ext, sbuf, rbuf, xbuf, xrec, own, early, xown, sown, delta, scale, state, ids,
-    gbuf, tbuf, sbuf_slot, i_sem, o_sem,
+    gbuf, tbuf, sbuf_slot, pbuf, i_sem, o_sem,
     w_send, w_recv, w_loc, a_send, a_recv, a_loc,
     g_send, g_recv, e_send, e_recv, r_send, r_recv, x_send, x_recv, pair,
 ):
@@ -65,6 +65,7 @@
         ),
         pltpu.make_async_copy(tgt, tbuf, i_sem.at[2]),
         pltpu.make_async_copy(slt, sbuf_slot, i_sem.at[3]),
+        pltpu.make_async_copy(plan, pbuf, i_sem.at[4]),
     ]
     for cp in inputs:
         cp.start()
@@ -159,11 +160,11 @@
             for i, k in enumerate(HOPS)
         ]
 
-    def ext_copies(g, par):
+    def ext_copies(g, par, peer=q_peer):
         return [
             remote(
                 ext.at[par, g, 0], ext.at[par, g, 4 - k],
-                e_send.at[par, g, i], e_recv.at[par, g, i], p_peer(k),
+                e_send.at[par, g, i], e_recv.at[par, g, i], peer(k),
             )
             for i, k in enumerate(HOPS)
         ]
@@ -177,11 +178,11 @@
             for i, k in enumerate(HOPS)
         ]
 
-    def inner_copies(g, par):
+    def inner_copies(g, par, peer=p_peer):
         return [
             remote(
                 xbuf.at[par, g], xrec.at[par, g, i],
-                x_send.at[par, g, i], x_recv.at[par, g, i], q_peer(k),
+                x_send.at[par, g, i], x_recv.at[par, g, i], peer(k),
             )
             for i, k in enumerate(HOPS)
         ]
@@ -200,7 +201,7 @@
         tail = jnp.where(line == 0, top, jnp.where(line == 1, square - top, 0.0))
         return inner.astype(BF), tail.astype(BF)
 
-    def send_inner(g, par):
+    def send_inner(g, par, peer=q_peer):
         now = state[group(g)].astype(F32)
         square = jnp.sum(now * now, axis=1, keepdims=True)
         square = jnp.sum(jnp.where(diagonal, square, 0.0), axis=0, keepdims=True)
@@ -219,7 +220,7 @@
         body, tail = packed(jnp.where(low, acc[:deep], acc[deep:]), square)
         ext[par, g, 0, 0:deep] = body
         ext[par, g, 0, deep:deep + 16] = tail
-        for cp in ext_copies(g, par):
+        for cp in ext_copies(g, par, peer):
             cp.start()
 
     def arrive(h, par):
@@ -258,7 +259,7 @@
             )
             send_near(h, par, early[part(h)] + last)
 
-    def forward(g, par):
+    def forward(g, par, peer=p_peer):
         for cp in ext_copies(g, par):
             cp.wait()
         both = ext[par, g, 0].astype(F32)
@@ -268,7 +269,7 @@
         body, tail = packed(inner, square)
         xbuf[par, g, 0:deep] = body
         xbuf[par, g, deep:deep + 16] = tail
-        for cp in inner_copies(g, par):
+        for cp in inner_copies(g, par, peer):
             cp.start()
         xown[g] = inner
         sown[g] = jnp.broadcast_to(square, (8, 128))
@@ -312,13 +313,6 @@
     def result(h):
         return pltpu.make_async_copy(state.at[part(h)], out.at[part(h)], o_sem.at[h])
 
-    inputs[0].wait()
-    inputs[1].wait()
-
-    @pl.loop(0, parts)
-    def _(h):
-        send_scaled(h, 0)
-
     for j in range(4):
         w_out[j].start()
     for j in range(4):
@@ -327,8 +321,16 @@
     for cp in w_keep:
         cp.start()
 
+    inputs[0].wait()
+    inputs[1].wait()
+
+    @pl.loop(0, parts)
+    def _(h):
+        send_scaled(h, 0)
+
     inputs[2].wait()
     inputs[3].wait()
+    inputs[4].wait()
     wanted = tbuf[...]
     place = sbuf_slot[...]
     key = wanted * 4 + place - 8
@@ -336,7 +338,7 @@
     for a in range(8):
         for r in range(4):
             hit = jnp.logical_and(place >= 8, key == a * 4 + r)
-            chosen = jnp.where(hit, plan[r, a], chosen)
+            chosen = jnp.where(hit, pbuf[r, a], chosen)
     chosen = chosen.astype(F32)
     upper = (lax.broadcasted_iota(jnp.int32, (block, 128), 1) >= 64).astype(F32)
     for g in range(groups):
@@ -380,7 +382,7 @@
 
     @pl.loop(0, groups)
     def _(g):
-        send_inner(g, 0)
+        send_inner(g, 0, p_peer)
 
     pass_on(u_here, u_on, u_across)
     pass_rest(u_here, u_across)
@@ -394,7 +396,7 @@
 
     @pl.loop(0, groups)
     def _(g):
-        forward(g, 0)
+        forward(g, 0, q_peer)
 
     pass_last(u_on, u_across)
     for j in range(3):
@@ -433,6 +435,8 @@
         @pl.when(t == 0)
         def _():
             settle(u_here, u_across, u_keep)
+            drain(d_here, d_on, d_across)
+            drain(u_here, u_on, u_across)
 
         @pl.loop(0, groups)
         def _(g):
@@ -455,8 +459,6 @@
             def _():
                 send_inner(g, 1 - par)
 
-    drain(d_here, d_on, d_across)
-    drain(u_here, u_on, u_across)
     for h in range(parts):
         result(h).wait()
 
@@ -477,7 +479,7 @@
         out_shape=jax.ShapeDtypeStruct((rows_all, width), BF),
         in_specs=[
             anywhere, anywhere, anywhere, anywhere, anywhere,
-            pl.BlockSpec(memory_space=pltpu.SMEM), anywhere, anywhere,
+            anywhere, anywhere, anywhere,
         ],
         out_specs=anywhere,
         scratch_shapes=[
@@ -501,7 +503,8 @@
             pltpu.VMEM((1, width), F32),
             pltpu.VMEM((1, rows_all), jnp.int32),
             pltpu.VMEM((1, rows_all), jnp.int32),
-            dma((4,)), dma((PARTS,)),
+            pltpu.SMEM((4, 8), jnp.int32),
+            dma((5,)), dma((PARTS,)),
             dma((3, 4)), dma((3, 4)), dma((4,)),
             dma((2, 13)), dma((2, 13)), dma((2,)),
             dma((2, PARTS, 3)), dma((2, PARTS, 3)),

time: 85.9 us -> 84.7 us (0.986)
  Pallas kernels: 83.1 us -> 82.2 us
where the time goes in v5:
time: 84.7 us; the launch traced here: 83.9 us
  Pallas kernels  82.2 us (97%)
  local copies, waits for them, and re-layouts  1.62 us (2%)
    pallas_call x1, Pallas kernels, local(): pl.pallas_call(functools.partial(kernel, PARTS, GROUPS), out_shape=jax.Sh...  82.2 us

profile of v5, /device:TPU:0, one launch (start us, length us, event | category | flops | bytes accessed | tf_op | source)
XLA Modules:
  0.0 83.9 jit_solution(13683001861794747333)
XLA Ops:
  0.0 82.2 %shard_map.82 = bf16[256,384]{1,0:T(8,128)(2,1)} custom-call(bf16[256,384]{1,0:T(8,128)(2,1)} %tok.1, f32[1,6144]{1,0:T(1,128)} %bitcast.8, bf16[6144,384]{1,0:T(8,128)(2,1)} %w.1, bf16[512,384]{1,0:T(8,128)(2,1)} %bitcast.6, bf16[512,384]{1,0:T(8,128)(2,1)} %bitcast.7, s32[4,8]{1,0:T(4,128)} %bitcast.9, s32[1,256]{1,0:T(1,128)} %bitcast.10, s32[1,256]{1,0:T(1,128)} %bitcast.11), custom_call_target="tpu_custom_call" | custom-call | tf_op jit(solution)/shard_map/pallas_call | solution.py:477
  82.2 1.6 %copy.10 = bf16[256,384]{1,0:T(8,128)(2,1)} copy(bf16[256,384]{1,0:T(8,128)(2,1)} %shard_map.82) | data formatting | bytes 393216

commit v6 on v5

--- a/solution.py
+++ b/solution.py
@@ -315,18 +315,19 @@
 
     for j in range(4):
         w_out[j].start()
+    for cp in w_keep:
+        cp.start()
+
+    inputs[0].wait()
+    inputs[1].wait()
+
+    @pl.loop(0, parts)
+    def _(h):
+        send_scaled(h, 0)
+
     for j in range(4):
         for i in (1, 2):
             w_out[i * 4 + j].start()
-    for cp in w_keep:
-        cp.start()
-
-    inputs[0].wait()
-    inputs[1].wait()
-
-    @pl.loop(0, parts)
-    def _(h):
-        send_scaled(h, 0)
 
     inputs[2].wait()
     inputs[3].wait()
@@ -418,8 +419,11 @@
     @pl.loop(0, STEPS)
     def _(t):
         par = t % 2
-        pl.semaphore_signal(pair, inc=1, device_id=mate, device_id_type=MESH)
-        pl.semaphore_wait(pair, 1)
+
+        @pl.when(t > 0)
+        def _():
+            pl.semaphore_signal(pair, inc=1, device_id=mate, device_id_type=MESH)
+            pl.semaphore_wait(pair, 1)
 
         @pl.loop(0, groups)
         def _(g):
@@ -437,6 +441,11 @@
             settle(u_here, u_across, u_keep)
             drain(d_here, d_on, d_across)
             drain(u_here, u_on, u_across)
+
+        @pl.when(t > 0)
+        def _():
+            pl.semaphore_signal(pair, inc=1, device_id=mate, device_id_type=MESH)
+            pl.semaphore_wait(pair, 1)
 
         @pl.loop(0, groups)
         def _(g):

time: 84.7 us -> 83.7 us (0.988)
  no operation moved by 1% of the time
where the time goes in v6:
time: 83.7 us; the launch traced here: 83.6 us
  Pallas kernels  82 us (98%)
  local copies, waits for them, and re-layouts  1.62 us (2%)
    pallas_call x1, Pallas kernels, local(): pl.pallas_call(functools.partial(kernel, PARTS, GROUPS), out_shape=jax.Sh...  82 us

profile of v6, /device:TPU:0, one launch (start us, length us, event | category | flops | bytes accessed | tf_op | source)
XLA Modules:
  0.0 83.6 jit_solution(7895456774528883147)
XLA Ops:
  0.0 82.0 %shard_map.82 = bf16[256,384]{1,0:T(8,128)(2,1)} custom-call(bf16[256,384]{1,0:T(8,128)(2,1)} %tok.1, f32[1,6144]{1,0:T(1,128)} %bitcast.8, bf16[6144,384]{1,0:T(8,128)(2,1)} %w.1, bf16[512,384]{1,0:T(8,128)(2,1)} %bitcast.6, bf16[512,384]{1,0:T(8,128)(2,1)} %bitcast.7, s32[4,8]{1,0:T(4,128)} %bitcast.9, s32[1,256]{1,0:T(1,128)} %bitcast.10, s32[1,256]{1,0:T(1,128)} %bitcast.11), custom_call_target="tpu_custom_call" | custom-call | tf_op jit(solution)/shard_map/pallas_call | solution.py:486
  82.0 1.6 %copy.10 = bf16[256,384]{1,0:T(8,128)(2,1)} copy(bf16[256,384]{1,0:T(8,128)(2,1)} %shard_map.82) | data formatting | bytes 393216

commit v7 on v6

--- a/solution.py
+++ b/solution.py
@@ -386,7 +386,6 @@
         send_inner(g, 0, p_peer)
 
     pass_on(u_here, u_on, u_across)
-    pass_rest(u_here, u_across)
     for cp in w_keep + w_out[:4]:
         cp.wait()
 
@@ -399,6 +398,7 @@
     def _(g):
         forward(g, 0, q_peer)
 
+    pass_rest(u_here, u_across)
     pass_last(u_on, u_across)
     for j in range(3):
         w_out[4 + j].wait()

time: 83.7 us -> 83.7 us (level)
  no operation moved by 1% of the time
where the time goes in v7:
time: 83.7 us; the launch traced here: 83.6 us
  Pallas kernels  82 us (98%)
  local copies, waits for them, and re-layouts  1.62 us (2%)
    pallas_call x1, Pallas kernels, local(): pl.pallas_call(functools.partial(kernel, PARTS, GROUPS), out_shape=jax.Sh...  82 us

profile of v7, /device:TPU:0, one launch (start us, length us, event | category | flops | bytes accessed | tf_op | source)
XLA Modules:
  0.0 83.6 jit_solution(3003608403507594553)
XLA Ops:
  0.0 82.0 %shard_map.82 = bf16[256,384]{1,0:T(8,128)(2,1)} custom-call(bf16[256,384]{1,0:T(8,128)(2,1)} %tok.1, f32[1,6144]{1,0:T(1,128)} %bitcast.8, bf16[6144,384]{1,0:T(8,128)(2,1)} %w.1, bf16[512,384]{1,0:T(8,128)(2,1)} %bitcast.6, bf16[512,384]{1,0:T(8,128)(2,1)} %bitcast.7, s32[4,8]{1,0:T(4,128)} %bitcast.9, s32[1,256]{1,0:T(1,128)} %bitcast.10, s32[1,256]{1,0:T(1,128)} %bitcast.11), custom_call_target="tpu_custom_call" | custom-call | tf_op jit(solution)/shard_map/pallas_call | solution.py:486
  82.0 1.6 %copy.10 = bf16[256,384]{1,0:T(8,128)(2,1)} copy(bf16[256,384]{1,0:T(8,128)(2,1)} %shard_map.82) | data formatting | bytes 393216

commit v8 on v7

--- a/solution.py
+++ b/solution.py
@@ -245,6 +245,12 @@
         @pl.when(jnp.logical_not(first))
         def _():
             arrive(h, par)
+
+            @pl.when(h == 0)
+            def _():
+                pl.semaphore_signal(pair, inc=1, device_id=mate, device_id_type=MESH)
+                pl.semaphore_wait(pair, 1)
+
             far(h, par)
             send_near(
                 h, par,
@@ -419,11 +425,6 @@
     @pl.loop(0, STEPS)
     def _(t):
         par = t % 2
-
-        @pl.when(t > 0)
-        def _():
-            pl.semaphore_signal(pair, inc=1, device_id=mate, device_id_type=MESH)
-            pl.semaphore_wait(pair, 1)
 
         @pl.loop(0, groups)
         def _(g):

time: 83.7 us -> 83.8 us (level)
  no operation moved by 1% of the time
where the time goes in v8:
time: 83.8 us; the launch traced here: 83.7 us
  Pallas kernels  82.1 us (98%)
  local copies, waits for them, and re-layouts  1.62 us (2%)
    pallas_call x1, Pallas kernels, local(): pl.pallas_call(functools.partial(kernel, PARTS, GROUPS), out_shape=jax.Sh...  82.1 us

profile of v8, /device:TPU:0, one launch (start us, length us, event | category | flops | bytes accessed | tf_op | source)
XLA Modules:
  0.0 83.7 jit_solution(6622683237895221065)
XLA Ops:
  0.0 82.1 %shard_map.82 = bf16[256,384]{1,0:T(8,128)(2,1)} custom-call(bf16[256,384]{1,0:T(8,128)(2,1)} %tok.1, f32[1,6144]{1,0:T(1,128)} %bitcast.8, bf16[6144,384]{1,0:T(8,128)(2,1)} %w.1, bf16[512,384]{1,0:T(8,128)(2,1)} %bitcast.6, bf16[512,384]{1,0:T(8,128)(2,1)} %bitcast.7, s32[4,8]{1,0:T(4,128)} %bitcast.9, s32[1,256]{1,0:T(1,128)} %bitcast.10, s32[1,256]{1,0:T(1,128)} %bitcast.11), custom_call_target="tpu_custom_call" | custom-call | tf_op jit(solution)/shard_map/pallas_call | solution.py:487
  82.1 1.6 %copy.10 = bf16[256,384]{1,0:T(8,128)(2,1)} copy(bf16[256,384]{1,0:T(8,128)(2,1)} %shard_map.82) | data formatting | bytes 393216
